TPU v7x, 32 devices: a whole 2x2x4 slice. The times are simulated.
32 devices in a mesh: ia: 4 (over x, core), ja: 2 (over y), ka: 4 (over z).
Axes of the slice: x: 2, y: 2, z: 4, core: 2. Of those that a mesh axis runs over, the one named last changes fastest.
Arguments:
- tensor: float32 [128, 256, 512], P('ia', 'ja', 'ka'), may hold values from -200 to 200
- factor_b: float32 [256, 4, 96], P(('ja', 'ka')), may hold values from -4 to 4
- factor_c: float32 [512, 4, 96], P(('ka', 'ja')), may hold values from -4 to 4
Outputs:
- factor_a: float32 [128, 4, 96], P(('ia', 'ja', 'ka'))
- weights: float32 [4, 96], replicated
All inputs are finite; a program needn't handle non-finite values.
Results may differ from a plain program's by a relative error of at most 0.0003.
Values sent between devices are 32-bit elements; how exact they have to be, the bound alone decides.
A program may use at most 64 MiB of HBM per device.

v0:
```python
import jax
import jax.numpy as jnp
from jax import lax
from jax.sharding import PartitionSpec as P

highest = lax.Precision.HIGHEST


def gram_of(rows):
    return jnp.einsum(
        "jsr,jsq->srq", rows, rows, precision=highest, preferred_element_type=jnp.float32
    )


def solve_normal(rows, gram_b, gram_c):
    columns = []
    for member in range(rows.shape[1]):
        normal_mat = gram_b[member] * gram_c[member]
        factor_l = jnp.linalg.cholesky(normal_mat)
        right_side = rows[:, member, :].T
        lower_sol = lax.linalg.triangular_solve(factor_l, right_side, left_side=True, lower=True)
        upper_sol = lax.linalg.triangular_solve(
            factor_l, lower_sol, left_side=True, lower=True, transpose_a=True
        )
        columns.append(upper_sol.T)
    return jnp.stack(columns, axis=1)


def shards(tensor, factor_b, factor_c):
    rows_i, rows_j, rows_k = tensor.shape
    starts, col_count = (factor_b.shape[1], factor_b.shape[2])
    width = starts * col_count
    c_block = lax.all_gather(factor_c, "ja", axis=0, tiled=True)
    partial_value = jnp.dot(
        tensor.reshape(rows_i * rows_j, rows_k),
        c_block.reshape(rows_k, width),
        precision=highest,
        preferred_element_type=jnp.float32,
    ).reshape(rows_i, rows_j, width)
    piece = lax.all_gather(factor_b, "ka", axis=0, tiled=True)
    gram_sum = jnp.zeros((starts, col_count, col_count), jnp.float32)
    count = piece.shape[0]
    flat_rows = piece.reshape(count, width)
    mttkrp = jnp.einsum(
        "ijr,jr->ir",
        partial_value,
        flat_rows,
        precision=highest,
        preferred_element_type=jnp.float32,
    )
    mttkrp, gram_rows = (mttkrp, gram_sum)
    gram_b, gram_c = lax.psum((gram_of(factor_b), gram_of(factor_c)), ("ja", "ka"))
    owned = lax.psum_scatter(mttkrp, ("ja", "ka"), scatter_dimension=0, tiled=True)
    owned = owned.reshape(owned.shape[0], starts, col_count)
    factor_raw = solve_normal(owned, gram_b, gram_c)
    squares = jnp.sum(factor_raw * factor_raw, axis=0)
    total = lax.psum(squares, ("ia", "ja", "ka"))
    row_total = rows_i * lax.axis_size("ia")
    weights = jnp.sqrt(total / row_total + 1e-06)
    return (factor_raw / weights[None], weights)


def solution(mesh):
    in_specs = (P("ia", "ja", "ka"), P(("ja", "ka"), None, None), P(("ka", "ja"), None, None))
    out_specs = (P(("ia", "ja", "ka"), None, None), P())
    return jax.shard_map(shards, mesh=mesh, in_specs=in_specs, out_specs=out_specs, check_vma=False)
```

profile of v0, /device:TPU:0, one launch (start us, length us, event | category | flops | bytes accessed | tf_op | source)
XLA Modules:
  0.0 222.9 jit_solution(2822683292989447386)
XLA Ops:
  7.2 0.0 copy-start
  7.2 0.0 all-reduce.4.cloned.1.call-start
  7.2 2.3 %fusion = f32[4,96,96]{1,2,0:T(8,128)} fusion(f32[64,4,96]{2,1,0:T(4,128)} %param.10), kind=kOutput, calls=%fused_computation.4 | convolution fusion | flops 28311552 | bytes 245760 | tf_op jit(solution)/shard_map/jsr,jsq->srq/dot_general | solution.py:10
  9.5 2.1 fusion.2
  11.6 0.0 all-reduce.4.cloned.1.call-update
  11.6 7.4 %all_gather.6 = f32[128,4,96]{2,1,0:T(4,128)S(1)} all-gather(f32[64,4,96]{2,1,0:T(4,128)} %param.10), channel_id=1, replica_groups=mesh['ia'=4,'ja'=2,'ka'=4] {'ja'}, dimensions={0}, use_global_device_ids=true | all-gather | bytes 294912 | tf_op jit(solution)/shard_map/all_gather | solution.py:33
  19.1 15.1 %all_gather.7 = f32[128,4,96]{2,1,0:T(4,128)S(1)} all-gather(f32[32,4,96]{2,1,0:T(4,128)} %param.9), channel_id=1, replica_groups=mesh['ia'=4,'ja'=2,'ka'=4] {'ka'}, dimensions={0}, use_global_device_ids=true | all-gather | bytes 245760 | tf_op jit(solution)/shard_map/all_gather | solution.py:40
  34.1 0.1 copy.36
  34.2 0.0 copy-done
  34.3 7.1 %fusion.28 = f32[32,128,384]{2,1,0:T(8,128)} fusion(f32[32,128,128]{2,1,0:T(8,128)S(1)} %copy-done, f32[128,384,1]{0,1,2:T(8,128)S(1)} %bitcast.130), kind=kOutput, calls=%fused_computation.63 | convolution fusion | flops 2415919104 | bytes 8585216 | tf_op jit(solution)/shard_map/dot_general | solution.py:34
  41.3 6.7 %copy.46 = f32[32,128,384]{1,0,2:T(8,128)} copy(f32[32,128,384]{2,1,0:T(8,128)} %fusion.28) | data formatting | bytes 12582912 | tf_op jit(solution)/shard_map/dot_general | solution.py:34
  48.0 0.0 copy-start.2
  48.0 0.1 copy.38
  48.2 11.9 %fusion.29 = f32[384,1,32]{2,1,0:T(1,128)S(1)} fusion(f32[32,128,384]{1,0,2:T(8,128)} %copy.46, f32[128,384,1]{0,2,1:T(1,128)S(1)} %bitcast.124), kind=kOutput, calls=%fused_computation.64 | convolution fusion | flops 18874368 | bytes 6537216 | tf_op jit(solution)/shard_map/ijr,jr->ir/dot_general | solution.py:44
  60.0 0.0 copy-done.2
  60.0 0.6 dynamic-slice
  61.3 41.9 %all-reduce = f32[32,384]{0,1:T(8,128)S(1)} all-reduce(f32[32,384]{0,1:T(8,128)S(1)} %bitcast.125), channel_id=2, replica_groups=mesh['ia'=4,'ja'=2,'ka'=4] {'ja','ka'}, use_global_device_ids=true, to_apply=%region_4.0.clone | all-reduce | flops 12288 | bytes 98304
  103.2 0.1 constant_dynamic-slice_fusion
  103.3 0.0 all-reduce.4.cloned.1.call-done
  103.4 1.0 fusion.24
  104.4 0.1 copy.35
  104.4 0.1 copy.41
  104.5 0.1 copy.40
  104.6 0.1 copy.39
  104.7 1.0 fusion.15
  105.7 8.8 %cholesky.107 = f32[96,96]{1,0:T(8,128)S(1)} custom-call(f32[96,96]{1,0:T(8,128)S(1)} %get-tuple-element.14), custom_call_target="Cholesky" | custom-call | tf_op jit(solution)/shard_map/jit(cholesky)/cholesky | solution.py:19
  114.5 0.6 compare_reduce_fusion
  115.2 0.7 fusion.7
  115.9 7.4 %custom-call.21 = f32[1,96,96]{1,2,0:T(8,128)S(1)} custom-call(f32[1,96,96]{2,1,0:T(8,128)S(1)} %fusion.7), custom_call_target="InvertDiagBlocksLowerTriangular" | custom-call | tf_op jit(solution)/shard_map/triangular_solve/custom-call.2 | solution.py:22
  123.2 0.2 fusion.8
  123.4 0.2 convolution_bitcast_fusion
  123.6 8.8 %cholesky.96 = f32[96,96]{1,0:T(8,128)S(1)} custom-call(f32[96,96]{1,0:T(8,128)S(1)} %get-tuple-element.15), custom_call_target="Cholesky" | custom-call | tf_op jit(solution)/shard_map/jit(cholesky)/cholesky | solution.py:19
  132.5 0.6 compare_reduce_fusion.1
  133.1 0.7 fusion.6
  133.8 7.4 %custom-call.19 = f32[1,96,96]{1,2,0:T(8,128)S(1)} custom-call(f32[1,96,96]{2,1,0:T(8,128)S(1)} %fusion.6), custom_call_target="InvertDiagBlocksLowerTriangular" | custom-call | tf_op jit(solution)/shard_map/triangular_solve/custom-call.2 | solution.py:22
  141.1 0.2 fusion.9
  141.3 0.2 convolution_bitcast_fusion.1
  141.5 8.8 %cholesky.85 = f32[96,96]{1,0:T(8,128)S(1)} custom-call(f32[96,96]{1,0:T(8,128)S(1)} %get-tuple-element.16), custom_call_target="Cholesky" | custom-call | tf_op jit(solution)/shard_map/jit(cholesky)/cholesky | solution.py:19
  150.4 0.6 compare_reduce_fusion.2
  151.0 0.7 fusion.5
  151.7 7.4 %custom-call.17 = f32[1,96,96]{1,2,0:T(8,128)S(1)} custom-call(f32[1,96,96]{2,1,0:T(8,128)S(1)} %fusion.5), custom_call_target="InvertDiagBlocksLowerTriangular" | custom-call | tf_op jit(solution)/shard_map/triangular_solve/custom-call.2 | solution.py:22
  159.1 0.2 fusion.10
  159.3 0.2 convolution_bitcast_fusion.2
  159.5 9.0 %cholesky.74 = f32[96,96]{1,0:T(8,128)S(1)} custom-call(f32[96,96]{1,0:T(8,128)S(1)} %get-tuple-element.13), custom_call_target="Cholesky" | custom-call | tf_op jit(solution)/shard_map/jit(cholesky)/cholesky | solution.py:19
  168.5 0.6 compare_reduce_fusion.3
  169.2 0.7 fusion.4
  169.8 7.4 %custom-call.15 = f32[1,96,96]{1,2,0:T(8,128)S(1)} custom-call(f32[1,96,96]{2,1,0:T(8,128)S(1)} %fusion.4), custom_call_target="InvertDiagBlocksLowerTriangular" | custom-call | tf_op jit(solution)/shard_map/triangular_solve/custom-call.2 | solution.py:22
  177.2 0.2 fusion.11
  177.4 0.2 convolution_bitcast_fusion.3
  177.6 0.1 multiply_reduce_fusion
  177.6 37.8 %psum.23 = f32[4,96]{1,0:T(4,128)S(1)} all-reduce(f32[4,96]{1,0:T(4,128)S(1)} %multiply_reduce_fusion), channel_id=1, replica_groups=mesh['ia'=4,'ja'=2,'ka'=4] {'ia','ja','ka'}, use_global_device_ids=true, to_apply=%region_6.10 | all-reduce | flops 384 | bytes 3072 | tf_op jit(solution)/shard_map/psum | solution.py:57
  215.4 0.0 copy-start.1
  215.5 0.6 copy.42
  216.1 0.0 copy-done.1
  (6 shorter events, 0.1 us)
Async XLA Ops:
  7.2 27.1 %copy-start = (f32[32,128,128]{2,1,0:T(8,128)S(1)}, f32[32,128,128]{2,1,0:T(8,128)}, u32[]{:S(2)}) copy-start(f32[32,128,128]{2,1,0:T(8,128)} %param.8) | copy-start | bytes 6291460
  7.2 96.2 %all-reduce.4.cloned.1.call-start = ((), (), s32[]{:S(2)}) async-start(), calls=%async_computation | async-start | bytes 786432 | tf_op jit(solution)/shard_map/psum | solution.py:52
  48.0 12.0 %copy-start.2 = (u32[32]{0:T(128)S(1)}, u32[32]{0:T(128)}, u32[]{:S(2)}) copy-start(u32[32]{0:T(128)} %constant.41) | copy-start | bytes 388
  215.4 0.6 copy-start.1
Sparse Core Ops, SparseCore 0:
  11.8 75.5 all-reduce.3
where the time goes:
time: 223 us
  blocking collectives  102 us (46%)
  other arithmetic  72.3 us (32%)
  matrix products  24.9 us (11%)
  between operations  14.9 us (7%)
  local copies, waits for them, and re-layouts  8.59 us (4%)
    unnamed x1, blocking collectives  41.9 us
    another operation x12, other arithmetic, solve_normal(): factor_l = jnp.linalg.cholesky(normal_mat)  38.1 us
    psum x1, blocking collectives, shards(): total = lax.psum(squares, ('ia', 'ja', 'ka'))  37.8 us
    another operation x8, other arithmetic, solve_normal(): lax.linalg.triangular_solve(factor_l, lower_sol, left_side=True, lower=Tr...  32 us
    all_gather x1, blocking collectives, shards(): piece = lax.all_gather(factor_b, 'ka', axis=0, tiled=True)  15.1 us
    dot_general x1, matrix products, shards(): jnp.einsum('ijr,jr->ir', partial_value, flat_rows, precision=highest, pre...  11.9 us
    all_gather x1, blocking collectives, shards(): c_block = lax.all_gather(factor_c, 'ja', axis=0, tiled=True)  7.42 us
    dot_general x1, matrix products, shards(): jnp.dot(tensor.reshape(rows_i * rows_j, rows_k), c_block.reshape(rows_k,...  7.07 us
  transfers between devices with their start and end apart: 1, of which 0 were waited for; matrix products, arithmetic and copies ran while one was open for 12% of the time, Pallas kernels for 0%

commit v1 on v0

--- a/solution.py
+++ b/solution.py
@@ -54,7 +54,8 @@
     owned = owned.reshape(owned.shape[0], starts, col_count)
     factor_raw = solve_normal(owned, gram_b, gram_c)
     squares = jnp.sum(factor_raw * factor_raw, axis=0)
-    total = lax.psum(squares, ("ia", "ja", "ka"))
+    one_axis = lax.psum(squares, ("ja", "ka"))
+    total = lax.psum(one_axis, "ia")
     row_total = rows_i * lax.axis_size("ia")
     weights = jnp.sqrt(total / row_total + 1e-06)
     return (factor_raw / weights[None], weights)

time: 223 us -> 208 us (0.933)
  blocking collectives: 102 us -> 87.3 us
    psum x1 -> x2, blocking collectives: 37.8 us -> 22.9 us  [the longest x1 17.2 us: shards(): one_axis = lax.psum(squares, ('ja', 'ka'))]
  transfers between devices with their start and end apart: 1 -> 1, of which waited for: 0 -> 0; matrix products, arithmetic and copies ran while one was open for 12% -> 13% of each run, Pallas kernels for 0% -> 0%
where the time goes in v1:
time: 208 us
  blocking collectives  87.3 us (42%)
  other arithmetic  72.3 us (35%)
  matrix products  24.9 us (12%)
  between operations  14.9 us (7%)
  local copies, waits for them, and re-layouts  8.6 us (4%)
    unnamed x1, blocking collectives  41.9 us
    another operation x12, other arithmetic, solve_normal(): factor_l = jnp.linalg.cholesky(normal_mat)  38.1 us
    another operation x8, other arithmetic, solve_normal(): lax.linalg.triangular_solve(factor_l, lower_sol, left_side=True, lower=Tr...  32 us
    psum x1, blocking collectives, shards(): one_axis = lax.psum(squares, ('ja', 'ka'))  17.2 us
    all_gather x1, blocking collectives, shards(): piece = lax.all_gather(factor_b, 'ka', axis=0, tiled=True)  15.1 us
    dot_general x1, matrix products, shards(): jnp.einsum('ijr,jr->ir', partial_value, flat_rows, precision=highest, pre...  11.9 us
    all_gather x1, blocking collectives, shards(): c_block = lax.all_gather(factor_c, 'ja', axis=0, tiled=True)  7.42 us
    dot_general x1, matrix products, shards(): jnp.dot(tensor.reshape(rows_i * rows_j, rows_k), c_block.reshape(rows_k,...  7.07 us
  transfers between devices with their start and end apart: 1, of which 0 were waited for; matrix products, arithmetic and copies ran while one was open for 13% of the time, Pallas kernels for 0%

profile of v1, /device:TPU:0, one launch (start us, length us, event | category | flops | bytes accessed | tf_op | source)
XLA Modules:
  0.0 208.0 jit_solution(1358652794117732678)
XLA Ops:
  7.2 0.0 copy-start
  7.2 0.0 all-reduce.4.cloned.1.call-start
  7.2 2.3 %fusion = f32[4,96,96]{1,2,0:T(8,128)} fusion(f32[64,4,96]{2,1,0:T(4,128)} %param.10), kind=kOutput, calls=%fused_computation.4 | convolution fusion | flops 28311552 | bytes 245760 | tf_op jit(solution)/shard_map/jsr,jsq->srq/dot_general | solution.py:10
  9.5 2.1 %fusion.2 = f32[4,96,96]{1,2,0:T(8,128)} fusion(f32[32,4,96]{2,1,0:T(4,128)} %param.9), kind=kOutput, calls=%fused_computation.6 | convolution fusion | flops 14155776 | bytes 196608 | tf_op jit(solution)/shard_map/jsr,jsq->srq/dot_general | solution.py:10
  11.6 0.0 all-reduce.4.cloned.1.call-update
  11.6 7.4 %all_gather.6 = f32[128,4,96]{2,1,0:T(4,128)S(1)} all-gather(f32[64,4,96]{2,1,0:T(4,128)} %param.10), channel_id=1, replica_groups=mesh['ia'=4,'ja'=2,'ka'=4] {'ja'}, dimensions={0}, use_global_device_ids=true | all-gather | bytes 294912 | tf_op jit(solution)/shard_map/all_gather | solution.py:33
  19.1 15.1 %all_gather.7 = f32[128,4,96]{2,1,0:T(4,128)S(1)} all-gather(f32[32,4,96]{2,1,0:T(4,128)} %param.9), channel_id=1, replica_groups=mesh['ia'=4,'ja'=2,'ka'=4] {'ka'}, dimensions={0}, use_global_device_ids=true | all-gather | bytes 245760 | tf_op jit(solution)/shard_map/all_gather | solution.py:40
  34.1 0.1 copy.36
  34.2 0.0 copy-done
  34.3 7.1 %fusion.28 = f32[32,128,384]{2,1,0:T(8,128)} fusion(f32[32,128,128]{2,1,0:T(8,128)S(1)} %copy-done, f32[128,384,1]{0,1,2:T(8,128)S(1)} %bitcast.130), kind=kOutput, calls=%fused_computation.63 | convolution fusion | flops 2415919104 | bytes 8585216 | tf_op jit(solution)/shard_map/dot_general | solution.py:34
  41.3 6.7 %copy.46 = f32[32,128,384]{1,0,2:T(8,128)} copy(f32[32,128,384]{2,1,0:T(8,128)} %fusion.28) | data formatting | bytes 12582912 | tf_op jit(solution)/shard_map/dot_general | solution.py:34
  48.0 0.0 copy-start.2
  48.0 0.1 copy.38
  48.2 11.9 %fusion.29 = f32[384,1,32]{2,1,0:T(1,128)S(1)} fusion(f32[32,128,384]{1,0,2:T(8,128)} %copy.46, f32[128,384,1]{0,2,1:T(1,128)S(1)} %bitcast.124), kind=kOutput, calls=%fused_computation.64 | convolution fusion | flops 18874368 | bytes 6537216 | tf_op jit(solution)/shard_map/ijr,jr->ir/dot_general | solution.py:44
  60.0 0.0 copy-done.2
  60.0 0.6 dynamic-slice
  61.3 41.9 %all-reduce = f32[32,384]{0,1:T(8,128)S(1)} all-reduce(f32[32,384]{0,1:T(8,128)S(1)} %bitcast.125), channel_id=2, replica_groups=mesh['ia'=4,'ja'=2,'ka'=4] {'ja','ka'}, use_global_device_ids=true, to_apply=%region_4.0.clone | all-reduce | flops 12288 | bytes 98304
  103.2 0.1 constant_dynamic-slice_fusion
  103.3 0.0 all-reduce.4.cloned.1.call-done
  103.4 1.0 fusion.24
  104.4 0.1 copy.35
  104.4 0.1 copy.41
  104.5 0.1 copy.40
  104.6 0.1 copy.39
  104.7 1.0 fusion.15
  105.7 8.8 %cholesky.107 = f32[96,96]{1,0:T(8,128)S(1)} custom-call(f32[96,96]{1,0:T(8,128)S(1)} %get-tuple-element.14), custom_call_target="Cholesky" | custom-call | tf_op jit(solution)/shard_map/jit(cholesky)/cholesky | solution.py:19
  114.5 0.6 compare_reduce_fusion
  115.2 0.7 fusion.7
  115.9 7.4 %custom-call.21 = f32[1,96,96]{1,2,0:T(8,128)S(1)} custom-call(f32[1,96,96]{2,1,0:T(8,128)S(1)} %fusion.7), custom_call_target="InvertDiagBlocksLowerTriangular" | custom-call | tf_op jit(solution)/shard_map/triangular_solve/custom-call.2 | solution.py:22
  123.2 0.2 fusion.8
  123.4 0.2 convolution_bitcast_fusion
  123.6 8.8 %cholesky.96 = f32[96,96]{1,0:T(8,128)S(1)} custom-call(f32[96,96]{1,0:T(8,128)S(1)} %get-tuple-element.15), custom_call_target="Cholesky" | custom-call | tf_op jit(solution)/shard_map/jit(cholesky)/cholesky | solution.py:19
  132.5 0.6 compare_reduce_fusion.1
  133.1 0.7 fusion.6
  133.8 7.4 %custom-call.19 = f32[1,96,96]{1,2,0:T(8,128)S(1)} custom-call(f32[1,96,96]{2,1,0:T(8,128)S(1)} %fusion.6), custom_call_target="InvertDiagBlocksLowerTriangular" | custom-call | tf_op jit(solution)/shard_map/triangular_solve/custom-call.2 | solution.py:22
  141.1 0.2 fusion.9
  141.3 0.2 convolution_bitcast_fusion.1
  141.5 8.8 %cholesky.85 = f32[96,96]{1,0:T(8,128)S(1)} custom-call(f32[96,96]{1,0:T(8,128)S(1)} %get-tuple-element.16), custom_call_target="Cholesky" | custom-call | tf_op jit(solution)/shard_map/jit(cholesky)/cholesky | solution.py:19
  150.4 0.6 compare_reduce_fusion.2
  151.0 0.7 fusion.5
  151.7 7.4 %custom-call.17 = f32[1,96,96]{1,2,0:T(8,128)S(1)} custom-call(f32[1,96,96]{2,1,0:T(8,128)S(1)} %fusion.5), custom_call_target="InvertDiagBlocksLowerTriangular" | custom-call | tf_op jit(solution)/shard_map/triangular_solve/custom-call.2 | solution.py:22
  159.1 0.2 fusion.10
  159.3 0.2 convolution_bitcast_fusion.2
  159.5 9.0 %cholesky.74 = f32[96,96]{1,0:T(8,128)S(1)} custom-call(f32[96,96]{1,0:T(8,128)S(1)} %get-tuple-element.13), custom_call_target="Cholesky" | custom-call | tf_op jit(solution)/shard_map/jit(cholesky)/cholesky | solution.py:19
  168.5 0.6 compare_reduce_fusion.3
  169.2 0.7 fusion.4
  169.8 7.4 %custom-call.15 = f32[1,96,96]{1,2,0:T(8,128)S(1)} custom-call(f32[1,96,96]{2,1,0:T(8,128)S(1)} %fusion.4), custom_call_target="InvertDiagBlocksLowerTriangular" | custom-call | tf_op jit(solution)/shard_map/triangular_solve/custom-call.2 | solution.py:22
  177.2 0.2 fusion.11
  177.4 0.2 convolution_bitcast_fusion.3
  177.6 0.1 multiply_reduce_fusion
  177.6 17.2 %psum.30 = f32[4,96]{1,0:T(4,128)S(1)} all-reduce(f32[4,96]{1,0:T(4,128)S(1)} %multiply_reduce_fusion), channel_id=1, replica_groups=mesh['ia'=4,'ja'=2,'ka'=4] {'ja','ka'}, use_global_device_ids=true, to_apply=%region_6.10 | all-reduce | flops 384 | bytes 3072 | tf_op jit(solution)/shard_map/psum | solution.py:57
  194.9 5.6 %psum.31 = f32[4,96]{1,0:T(4,128)S(1)} all-reduce(f32[4,96]{1,0:T(4,128)S(1)} %psum.30), channel_id=1, replica_groups=mesh['ia'=4,'ja'=2,'ka'=4] {'ia'}, use_global_device_ids=true, to_apply=%region_7.11 | all-reduce | flops 384 | bytes 3072 | tf_op jit(solution)/shard_map/psum | solution.py:58
  200.5 0.0 copy-start.1
  200.5 0.6 copy.42
  201.1 0.0 copy-done.1
  (6 shorter events, 0.2 us)
Async XLA Ops:
  7.2 27.1 %copy-start = (f32[32,128,128]{2,1,0:T(8,128)S(1)}, f32[32,128,128]{2,1,0:T(8,128)}, u32[]{:S(2)}) copy-start(f32[32,128,128]{2,1,0:T(8,128)} %param.8) | copy-start | bytes 6291460
  7.2 96.2 %all-reduce.4.cloned.1.call-start = ((), (), s32[]{:S(2)}) async-start(), calls=%async_computation | async-start | bytes 786432 | tf_op jit(solution)/shard_map/psum | solution.py:52
  48.0 12.0 %copy-start.2 = (u32[32]{0:T(128)S(1)}, u32[32]{0:T(128)}, u32[]{:S(2)}) copy-start(u32[32]{0:T(128)} %constant.41) | copy-start | bytes 388
  200.5 0.6 copy-start.1
Sparse Core Ops, SparseCore 0:
  11.8 75.5 all-reduce.3
